TPU v7x, 32 devices: a whole 2x2x4 slice. The times are simulated.
32 devices in a mesh: expert: 8 (over y, x, core), token: 4 (over z).
Axes of the slice: x: 2, y: 2, z: 4, core: 2. Of those that a mesh axis runs over, the one named last changes fastest.
Arguments:
- activations: bfloat16 [16, 1024, 768], P('expert', 'token'), may hold values from -6 to 6
- routed: int32 [16, 1024], P('expert', 'token'), may hold values 0 or 1
- weights: bfloat16 [128, 768, 256], P(('expert', 'token')), may hold values from -6 to 6, as said below
- kept_mask: int32 [128, 768, 256], P(('expert', 'token')), may hold values 0 or 1
- step_counts: int32 [128], P(('expert', 'token')), may hold values from 1 to 7
- ridge_scale: float32 [128], P(('expert', 'token')), may hold values from 0.05 to 0.5
Outputs:
- rebuilt: float32 [128, 768, 256], P(('expert', 'token'))
- misfit: float32 [16], P('expert')
Inputs may be any that keep to these rules, and one draw needn't show every extreme that they name: `weights`: every entry's magnitude is at least 0.25.
All inputs are finite; a program needn't handle non-finite values. No bound on the sum of `routed` or of `kept_mask` on one device may be relied on, other than what follows from the above.
Results may differ from a plain program's by a relative error of at most 0.0003.
Values may be sent and summed in bfloat16 or wider, within the bound.
A program may use at most 64 MiB of HBM per device.

v0:
```python
import jax
import jax.numpy as jnp
from jax import lax
from jax.sharding import PartitionSpec as P

D = 2048
COLS = 256


def solve_task(gram_matrix, frobenius, task_weights, task_mask, task_count, task_ridge):
    float_weights = task_weights.astype(jnp.float32)
    float_mask = task_mask.astype(jnp.float32)
    damping = task_ridge * frobenius
    step_size = 1.0 / (frobenius + damping)

    def advance(turn_index, current):
        gradient = (
            jnp.dot(gram_matrix, current - float_weights, precision=lax.Precision.HIGHEST)
            + damping * current
        )
        return current - step_size * (float_mask * gradient)

    result = lax.fori_loop(0, task_count, advance, float_mask * float_weights)
    change = result - float_weights
    numerator = jnp.sum(change * jnp.dot(gram_matrix, change, precision=lax.Precision.HIGHEST))
    energy = jnp.sum(
        float_weights * jnp.dot(gram_matrix, float_weights, precision=lax.Precision.HIGHEST)
    )
    return (result, numerator, energy)


def on_device(activations, routed, weights, kept_mask, step_counts, ridge_scale):
    local_experts, row_count, features = activations.shape
    local_tasks = weights.shape[0]
    per_expert = D // COLS
    total_rows = row_count * lax.axis_size("token")
    own_slot = lax.axis_index("token") * local_tasks // per_expert
    masked = activations * routed[:, :, None].astype(jnp.bfloat16)
    own_rows = lax.dynamic_index_in_dim(
        lax.all_gather(masked, "token", axis=1, tiled=True), own_slot, 0, keepdims=False
    )
    gram_sum = lax.dot_general(
        own_rows, own_rows, (((0,), (0,)), ((), ())), preferred_element_type=jnp.float32
    )
    gram_matrix = gram_sum / total_rows
    frobenius = jnp.sqrt(jnp.sum(gram_matrix * gram_matrix))

    def one_task(task_args):
        task_weights, task_mask, task_count, task_ridge = task_args
        return solve_task(gram_matrix, frobenius, task_weights, task_mask, task_count, task_ridge)

    rebuilt, numerators, energies = lax.map(
        one_task, (weights, kept_mask, step_counts, ridge_scale)
    )
    picker = (jnp.arange(local_experts) == own_slot).astype(jnp.float32)
    expert_terms = lax.psum(picker * jnp.sum(numerators), "token")
    layer_energy = lax.psum(jnp.sum(energies), ("expert", "token"))
    expert_total = local_experts * lax.axis_size("expert")
    misfit = expert_terms / (layer_energy / expert_total + 1e-06)
    return (rebuilt, misfit)


def solution(mesh):
    placed = (
        P("expert", "token", None),
        P("expert", "token"),
        P(("expert", "token"), None, None),
        P(("expert", "token"), None, None),
        P(("expert", "token")),
        P(("expert", "token")),
    )
    return jax.shard_map(
        on_device,
        mesh=mesh,
        in_specs=placed,
        out_specs=(P(("expert", "token"), None, None), P("expert")),
        check_vma=False,
    )
```

profile of v0, /device:TPU:0, one launch (start us, length us, event | category | flops | bytes accessed | tf_op | source)
XLA Modules:
  0.0 320.7 jit_solution(10718532296523301616)
XLA Ops:
  10.2 66.2 %all-gather.2.cloned.1.call-done = bf16[2,1024,768]{2,1,0:T(8,128)(2,1)} async-done(((bf16[2,256,768]{2,1,0:T(8,128)(2,1)}), bf16[2,1024,768]{2,1,0:T(8,128)(2,1)}) %all-gather.2.cloned.1.call-update) | async-done | bytes 3145744 | tf_op jit(solution)/shard_map/all_gather | solution.py:40
  76.4 4.1 %multiply_reduce_fusion = (f32[]{:T(128)}, f32[768,768]{1,0:T(8,128)S(1)}) fusion(bf16[2,1024,768]{2,1,0:T(8,128)(2,1)} %all-gather.2.cloned.1.call-done, s32[]{:T(128)S(6)} %select_n.10), kind=kOutput, calls=%fused_computation.22 | convolution fusion | flops 1209729024 | bytes 3932168 | tf_op jit(solution)/shard_map/dot_general | solution.py:42
  81.1 163.0 %while.25 = (s32[]{:T(128)}, f32[4,768,256]{2,1,0:T(8,128)}, f32[4]{0:T(128)S(1)}, f32[4]{0:T(128)S(1)}, s32[4,768,256]{2,1,0:T(8,128)}, /*index=5*/bf16[4,768,2...) while((s32[]{:T(128)}, f32[4,768,256]{2,1,0:T(8,128)}, ...), condition=%wide.region_6.7_spmd, body=%wide.region_1.6_spmd.sunk | while | flops 5439750144 | bytes 29491652 | solution.py:52
  94.6 27.0 %while.26 = (s32[]{:T(128)}, f32[768,256]{0,1:T(8,128)S(1)}, s32[]{:T(128)}, f32[]{:T(128)}, f32[768,256]{0,1:T(8,128)}, /*index=5*/f32[768,768]{1,0:T(8,128)S(1)}, f32[]{:T(128)}, f32[768,256]{0,1:T(8,128)}, s32[]{:T(128)}) while((s32[]{:T(128)}, f32[768,256]{0,1:T(8,128)S(1)}, s32[]{:T(128)}, f32[]{:T(128)}, f32[768,256]{0,1:T(8,128)}, ...), condition=%wide.region_3.3_spmd, body=%wide.region_2.2_spmd.sunk | while | flops 1813118976 | bytes 7077989 | solution.py:23
  95.3 3.7 %fusion.38 = f32[768,256]{0,1:T(8,128)S(1)} fusion(f32[768,256]{0,1:T(8,128)S(1)} %copy.48, f32[768,256]{0,1:T(8,128)} %get-tuple-element.307, f32[768,768]{1,0:T(8,128)S(1)} %get-tuple-element.305, f32[768,256]{0,1:T(8,128)} %get-tuple-element.304, f32[]{:T(128)} %get-tuple-element.306, f32[]{:T(128)} %get-tuple-element.303), kind=kOutput, calls=%fused_computation.4.clone.1 | convolution fusion | flops 1813118976 | bytes 5505032 | tf_op jit(solution)/shard_map/while/body/eval_jaxpr/while/body/dot_general | solution.py:18
  99.7 3.7 %fusion.38 = f32[768,256]{0,1:T(8,128)S(1)} fusion(f32[768,256]{0,1:T(8,128)S(1)} %copy.48, f32[768,256]{0,1:T(8,128)} %get-tuple-element.307, f32[768,768]{1,0:T(8,128)S(1)} %get-tuple-element.305, f32[768,256]{0,1:T(8,128)} %get-tuple-element.304, f32[]{:T(128)} %get-tuple-element.306, f32[]{:T(128)} %get-tuple-element.303), kind=kOutput, calls=%fused_computation.4.clone.1 | convolution fusion | flops 1813118976 | bytes 5505032 | tf_op jit(solution)/shard_map/while/body/eval_jaxpr/while/body/dot_general | solution.py:18
  104.1 3.7 %fusion.38 = f32[768,256]{0,1:T(8,128)S(1)} fusion(f32[768,256]{0,1:T(8,128)S(1)} %copy.48, f32[768,256]{0,1:T(8,128)} %get-tuple-element.307, f32[768,768]{1,0:T(8,128)S(1)} %get-tuple-element.305, f32[768,256]{0,1:T(8,128)} %get-tuple-element.304, f32[]{:T(128)} %get-tuple-element.306, f32[]{:T(128)} %get-tuple-element.303), kind=kOutput, calls=%fused_computation.4.clone.1 | convolution fusion | flops 1813118976 | bytes 5505032 | tf_op jit(solution)/shard_map/while/body/eval_jaxpr/while/body/dot_general | solution.py:18
  108.5 3.7 %fusion.38 = f32[768,256]{0,1:T(8,128)S(1)} fusion(f32[768,256]{0,1:T(8,128)S(1)} %copy.48, f32[768,256]{0,1:T(8,128)} %get-tuple-element.307, f32[768,768]{1,0:T(8,128)S(1)} %get-tuple-element.305, f32[768,256]{0,1:T(8,128)} %get-tuple-element.304, f32[]{:T(128)} %get-tuple-element.306, f32[]{:T(128)} %get-tuple-element.303), kind=kOutput, calls=%fused_computation.4.clone.1 | convolution fusion | flops 1813118976 | bytes 5505032 | tf_op jit(solution)/shard_map/while/body/eval_jaxpr/while/body/dot_general | solution.py:18
  112.9 3.7 %fusion.38 = f32[768,256]{0,1:T(8,128)S(1)} fusion(f32[768,256]{0,1:T(8,128)S(1)} %copy.48, f32[768,256]{0,1:T(8,128)} %get-tuple-element.307, f32[768,768]{1,0:T(8,128)S(1)} %get-tuple-element.305, f32[768,256]{0,1:T(8,128)} %get-tuple-element.304, f32[]{:T(128)} %get-tuple-element.306, f32[]{:T(128)} %get-tuple-element.303), kind=kOutput, calls=%fused_computation.4.clone.1 | convolution fusion | flops 1813118976 | bytes 5505032 | tf_op jit(solution)/shard_map/while/body/eval_jaxpr/while/body/dot_general | solution.py:18
  117.3 3.7 %fusion.38 = f32[768,256]{0,1:T(8,128)S(1)} fusion(f32[768,256]{0,1:T(8,128)S(1)} %copy.48, f32[768,256]{0,1:T(8,128)} %get-tuple-element.307, f32[768,768]{1,0:T(8,128)S(1)} %get-tuple-element.305, f32[768,256]{0,1:T(8,128)} %get-tuple-element.304, f32[]{:T(128)} %get-tuple-element.306, f32[]{:T(128)} %get-tuple-element.303), kind=kOutput, calls=%fused_computation.4.clone.1 | convolution fusion | flops 1813118976 | bytes 5505032 | tf_op jit(solution)/shard_map/while/body/eval_jaxpr/while/body/dot_general | solution.py:18
  142.0 27.0 %while.26 = (s32[]{:T(128)}, f32[768,256]{0,1:T(8,128)S(1)}, s32[]{:T(128)}, f32[]{:T(128)}, f32[768,256]{0,1:T(8,128)}, /*index=5*/f32[768,768]{1,0:T(8,128)S(1)}, f32[]{:T(128)}, f32[768,256]{0,1:T(8,128)}, s32[]{:T(128)}) while((s32[]{:T(128)}, f32[768,256]{0,1:T(8,128)S(1)}, s32[]{:T(128)}, f32[]{:T(128)}, f32[768,256]{0,1:T(8,128)}, ...), condition=%wide.region_3.3_spmd, body=%wide.region_2.2_spmd.sunk | while | flops 1813118976 | bytes 7077989 | solution.py:23
  142.7 3.7 %fusion.38 = f32[768,256]{0,1:T(8,128)S(1)} fusion(f32[768,256]{0,1:T(8,128)S(1)} %copy.48, f32[768,256]{0,1:T(8,128)} %get-tuple-element.307, f32[768,768]{1,0:T(8,128)S(1)} %get-tuple-element.305, f32[768,256]{0,1:T(8,128)} %get-tuple-element.304, f32[]{:T(128)} %get-tuple-element.306, f32[]{:T(128)} %get-tuple-element.303), kind=kOutput, calls=%fused_computation.4.clone.1 | convolution fusion | flops 1813118976 | bytes 5505032 | tf_op jit(solution)/shard_map/while/body/eval_jaxpr/while/body/dot_general | solution.py:18
  147.1 3.7 %fusion.38 = f32[768,256]{0,1:T(8,128)S(1)} fusion(f32[768,256]{0,1:T(8,128)S(1)} %copy.48, f32[768,256]{0,1:T(8,128)} %get-tuple-element.307, f32[768,768]{1,0:T(8,128)S(1)} %get-tuple-element.305, f32[768,256]{0,1:T(8,128)} %get-tuple-element.304, f32[]{:T(128)} %get-tuple-element.306, f32[]{:T(128)} %get-tuple-element.303), kind=kOutput, calls=%fused_computation.4.clone.1 | convolution fusion | flops 1813118976 | bytes 5505032 | tf_op jit(solution)/shard_map/while/body/eval_jaxpr/while/body/dot_general | solution.py:18
  151.5 3.7 %fusion.38 = f32[768,256]{0,1:T(8,128)S(1)} fusion(f32[768,256]{0,1:T(8,128)S(1)} %copy.48, f32[768,256]{0,1:T(8,128)} %get-tuple-element.307, f32[768,768]{1,0:T(8,128)S(1)} %get-tuple-element.305, f32[768,256]{0,1:T(8,128)} %get-tuple-element.304, f32[]{:T(128)} %get-tuple-element.306, f32[]{:T(128)} %get-tuple-element.303), kind=kOutput, calls=%fused_computation.4.clone.1 | convolution fusion | flops 1813118976 | bytes 5505032 | tf_op jit(solution)/shard_map/while/body/eval_jaxpr/while/body/dot_general | solution.py:18
  160.2 3.7 %fusion.38 = f32[768,256]{0,1:T(8,128)S(1)} fusion(f32[768,256]{0,1:T(8,128)S(1)} %copy.48, f32[768,256]{0,1:T(8,128)} %get-tuple-element.307, f32[768,768]{1,0:T(8,128)S(1)} %get-tuple-element.305, f32[768,256]{0,1:T(8,128)} %get-tuple-element.304, f32[]{:T(128)} %get-tuple-element.306, f32[]{:T(128)} %get-tuple-element.303), kind=kOutput, calls=%fused_computation.4.clone.1 | convolution fusion | flops 1813118976 | bytes 5505032 | tf_op jit(solution)/shard_map/while/body/eval_jaxpr/while/body/dot_general | solution.py:18
  164.6 3.7 %fusion.38 = f32[768,256]{0,1:T(8,128)S(1)} fusion(f32[768,256]{0,1:T(8,128)S(1)} %copy.48, f32[768,256]{0,1:T(8,128)} %get-tuple-element.307, f32[768,768]{1,0:T(8,128)S(1)} %get-tuple-element.305, f32[768,256]{0,1:T(8,128)} %get-tuple-element.304, f32[]{:T(128)} %get-tuple-element.306, f32[]{:T(128)} %get-tuple-element.303), kind=kOutput, calls=%fused_computation.4.clone.1 | convolution fusion | flops 1813118976 | bytes 5505032 | tf_op jit(solution)/shard_map/while/body/eval_jaxpr/while/body/dot_general | solution.py:18
  189.3 13.8 %while.26 = (s32[]{:T(128)}, f32[768,256]{0,1:T(8,128)S(1)}, s32[]{:T(128)}, f32[]{:T(128)}, f32[768,256]{0,1:T(8,128)}, /*index=5*/f32[768,768]{1,0:T(8,128)S(1)}, f32[]{:T(128)}, f32[768,256]{0,1:T(8,128)}, s32[]{:T(128)}) while((s32[]{:T(128)}, f32[768,256]{0,1:T(8,128)S(1)}, s32[]{:T(128)}, f32[]{:T(128)}, f32[768,256]{0,1:T(8,128)}, ...), condition=%wide.region_3.3_spmd, body=%wide.region_2.2_spmd.sunk | while | flops 1813118976 | bytes 7077989 | solution.py:23
  190.0 3.7 %fusion.38 = f32[768,256]{0,1:T(8,128)S(1)} fusion(f32[768,256]{0,1:T(8,128)S(1)} %copy.48, f32[768,256]{0,1:T(8,128)} %get-tuple-element.307, f32[768,768]{1,0:T(8,128)S(1)} %get-tuple-element.305, f32[768,256]{0,1:T(8,128)} %get-tuple-element.304, f32[]{:T(128)} %get-tuple-element.306, f32[]{:T(128)} %get-tuple-element.303), kind=kOutput, calls=%fused_computation.4.clone.1 | convolution fusion | flops 1813118976 | bytes 5505032 | tf_op jit(solution)/shard_map/while/body/eval_jaxpr/while/body/dot_general | solution.py:18
  198.8 3.7 %fusion.38 = f32[768,256]{0,1:T(8,128)S(1)} fusion(f32[768,256]{0,1:T(8,128)S(1)} %copy.48, f32[768,256]{0,1:T(8,128)} %get-tuple-element.307, f32[768,768]{1,0:T(8,128)S(1)} %get-tuple-element.305, f32[768,256]{0,1:T(8,128)} %get-tuple-element.304, f32[]{:T(128)} %get-tuple-element.306, f32[]{:T(128)} %get-tuple-element.303), kind=kOutput, calls=%fused_computation.4.clone.1 | convolution fusion | flops 1813118976 | bytes 5505032 | tf_op jit(solution)/shard_map/while/body/eval_jaxpr/while/body/dot_general | solution.py:18
  223.5 13.8 %while.26 = (s32[]{:T(128)}, f32[768,256]{0,1:T(8,128)S(1)}, s32[]{:T(128)}, f32[]{:T(128)}, f32[768,256]{0,1:T(8,128)}, /*index=5*/f32[768,768]{1,0:T(8,128)S(1)}, f32[]{:T(128)}, f32[768,256]{0,1:T(8,128)}, s32[]{:T(128)}) while((s32[]{:T(128)}, f32[768,256]{0,1:T(8,128)S(1)}, s32[]{:T(128)}, f32[]{:T(128)}, f32[768,256]{0,1:T(8,128)}, ...), condition=%wide.region_3.3_spmd, body=%wide.region_2.2_spmd.sunk | while | flops 1813118976 | bytes 7077989 | solution.py:23
  224.2 3.7 %fusion.38 = f32[768,256]{0,1:T(8,128)S(1)} fusion(f32[768,256]{0,1:T(8,128)S(1)} %copy.48, f32[768,256]{0,1:T(8,128)} %get-tuple-element.307, f32[768,768]{1,0:T(8,128)S(1)} %get-tuple-element.305, f32[768,256]{0,1:T(8,128)} %get-tuple-element.304, f32[]{:T(128)} %get-tuple-element.306, f32[]{:T(128)} %get-tuple-element.303), kind=kOutput, calls=%fused_computation.4.clone.1 | convolution fusion | flops 1813118976 | bytes 5505032 | tf_op jit(solution)/shard_map/while/body/eval_jaxpr/while/body/dot_general | solution.py:18
  228.6 3.7 %fusion.38 = f32[768,256]{0,1:T(8,128)S(1)} fusion(f32[768,256]{0,1:T(8,128)S(1)} %copy.48, f32[768,256]{0,1:T(8,128)} %get-tuple-element.307, f32[768,768]{1,0:T(8,128)S(1)} %get-tuple-element.305, f32[768,256]{0,1:T(8,128)} %get-tuple-element.304, f32[]{:T(128)} %get-tuple-element.306, f32[]{:T(128)} %get-tuple-element.303), kind=kOutput, calls=%fused_computation.4.clone.1 | convolution fusion | flops 1813118976 | bytes 5505032 | tf_op jit(solution)/shard_map/while/body/eval_jaxpr/while/body/dot_general | solution.py:18
  246.0 11.4 %psum.14 = f32[2]{0:T(128)S(1)} all-reduce(f32[2]{0:T(128)S(1)} %compare_select_fusion), channel_id=1, replica_groups=mesh['expert'=8,'token'=4] {'token'}, use_global_device_ids=true, to_apply=%region_8.9 | all-reduce | flops 2 | bytes 16 | tf_op jit(solution)/shard_map/psum | solution.py:56
  257.4 55.3 %psum.15 = f32[]{:T(128)} all-reduce(f32[]{:T(128)} %reduce_sum.47), channel_id=1, replica_groups=mesh['expert'=8,'token'=4] {'expert','token'}, use_global_device_ids=true, to_apply=%region_10.11 | all-reduce | flops 1 | bytes 8 | tf_op jit(solution)/shard_map/psum | solution.py:57
  (104 shorter events, 96.2 us)
Async XLA Ops:
  7.2 69.2 %all-gather.2.cloned.1.call-start = ((), (), s32[]{:S(2)}) async-start(), calls=%async_computation | async-start | bytes 3932160 | tf_op jit(solution)/shard_map/all_gather | solution.py:40
  10.1 71.0 %copy-start.1 = (s32[4]{0:T(128)S(1)}, s32[4]{0:T(128)}, u32[]{:S(2)}) copy-start(s32[4]{0:T(128)} %param.14) | copy-start | bytes 52
  10.1 71.0 %copy-start.2 = (f32[4]{0:T(128)S(1)}, f32[4]{0:T(128)}, u32[]{:S(2)}) copy-start(f32[4]{0:T(128)} %param.15) | copy-start | bytes 52
  91.6 0.9 copy-start
  138.9 0.9 copy-start
  186.3 0.9 copy-start
  220.4 0.9 copy-start
Sparse Core Ops, SparseCore 0:
  10.2 66.1 all-gather.1
where the time goes:
time: 323 us; the launch traced here: 321 us
  matrix products  90.8 us (28%)
  blocking collectives  66.7 us (21%)
  waiting for transfers between devices  66.3 us (21%)
  local copies, waits for them, and re-layouts  47.1 us (15%)
  other arithmetic  17.6 us (5%)
  loops' own time  16.9 us (5%)
  between operations  15.4 us (5%)
    dot_general x18, matrix products, advance(): jnp.dot(gram_matrix, current - float_weights, precision=lax.Precision.HIG...  66.3 us
    all_gather x1, waiting for transfers between devices, on_device(): lax.all_gather(masked, 'token', axis=1, tiled=True)  66.2 us
    psum x1, blocking collectives, on_device(): layer_energy = lax.psum(jnp.sum(energies), ('expert', 'token'))  55.3 us
    dynamic_slice x24, local copies, waits for them, and re-layouts, on_device(): lax.map(one_task, (weights, kept_mask, step_counts, ridge_scale))  23.4 us
    dynamic_update_slice x16, local copies, waits for them, and re-layouts, on_device(): lax.map(one_task, (weights, kept_mask, step_counts, ridge_scale))  19.2 us
    another operation x4, loops' own time, solve_task(): result = lax.fori_loop(0, task_count, advance, float_mask * float_weights)  14.3 us
    dot_general x4, matrix products, solve_task(): jnp.dot(gram_matrix, change, precision=lax.Precision.HIGHEST)  11.5 us
    psum x1, blocking collectives, on_device(): expert_terms = lax.psum(picker * jnp.sum(numerators), 'token')  11.4 us
  transfers between devices with their start and end apart: 1, of which 1 were waited for; matrix products, arithmetic and copies ran while one was open for 0% of the time, Pallas kernels for 0%

commit v1 on v0

--- a/solution.py
+++ b/solution.py
@@ -5,6 +5,19 @@
 
 D = 2048
 COLS = 256
+
+
+def gather_around(shard, axis, dim):
+    size, index, rows = (lax.axis_size(axis), lax.axis_index(axis), shard.shape[dim])
+    right = [(i, (i + 1) % size) for i in range(size)]
+    result = jnp.zeros((*shard.shape[:dim], size * rows, *shard.shape[dim + 1 :]), shard.dtype)
+    current = shard
+    for turn in range(size):
+        owner = (index - turn) % size
+        result = lax.dynamic_update_slice_in_dim(result, current, owner * rows, axis=dim)
+        if turn < size - 1:
+            current = lax.ppermute(current, axis, right)
+    return result
 
 
 def solve_task(gram_matrix, frobenius, task_weights, task_mask, task_count, task_ridge):
@@ -37,7 +50,7 @@
     own_slot = lax.axis_index("token") * local_tasks // per_expert
     masked = activations * routed[:, :, None].astype(jnp.bfloat16)
     own_rows = lax.dynamic_index_in_dim(
-        lax.all_gather(masked, "token", axis=1, tiled=True), own_slot, 0, keepdims=False
+        gather_around(masked, "token", 1), own_slot, 0, keepdims=False
     )
     gram_sum = lax.dot_general(
         own_rows, own_rows, (((0,), (0,)), ((), ())), preferred_element_type=jnp.float32

time: 323 us -> 307 us (0.950)
  between operations: 15.4 us -> 1.93 us
  waiting for transfers between devices: 66.3 us -> 57.8 us
  local copies, waits for them, and re-layouts: 47.1 us -> 51.9 us
    all_gather x1 -> x0, waiting for transfers between devices: 66.2 us -> none  [on_device(): lax.all_gather(masked, 'token', axis=1, tiled=True)]
    ppermute x0 -> x3, waiting for transfers between devices: none -> 57.8 us  [gather_around(): current = lax.ppermute(current, axis, right)]
  transfers between devices with their start and end apart: 1 -> 3, of which waited for: 1 -> 3; matrix products, arithmetic and copies ran while one was open for 0% -> 1% of each run, Pallas kernels for 0% -> 0%
where the time goes in v1:
time: 307 us; the launch traced here: 305 us
  matrix products  90.8 us (30%)
  blocking collectives  66.4 us (22%)
  waiting for transfers between devices  57.8 us (19%)
  local copies, waits for them, and re-layouts  51.9 us (17%)
  loops' own time  16.9 us (6%)
  other arithmetic  16.6 us (5%)
  starting transfers between devices  3.08 us (1%)
    dot_general x18, matrix products, advance(): jnp.dot(gram_matrix, current - float_weights, precision=lax.Precision.HIG...  66.3 us
    psum x1, blocking collectives, on_device(): layer_energy = lax.psum(jnp.sum(energies), ('expert', 'token'))  58.1 us
    ppermute x3, waiting for transfers between devices, gather_around(): current = lax.ppermute(current, axis, right)  57.8 us
    dynamic_slice x24, local copies, waits for them, and re-layouts, on_device(): lax.map(one_task, (weights, kept_mask, step_counts, ridge_scale))  23.4 us
    dynamic_update_slice x16, local copies, waits for them, and re-layouts, on_device(): lax.map(one_task, (weights, kept_mask, step_counts, ridge_scale))  19.2 us
    another operation x4, loops' own time, solve_task(): result = lax.fori_loop(0, task_count, advance, float_mask * float_weights)  14.3 us
    dot_general x4, matrix products, solve_task(): jnp.dot(gram_matrix, change, precision=lax.Precision.HIGHEST)  11.5 us
    dot_general x4, matrix products, solve_task(): jnp.dot(gram_matrix, float_weights, precision=lax.Precision.HIGHEST)  8.88 us
  transfers between devices with their start and end apart: 3, of which 3 were waited for; matrix products, arithmetic and copies ran while one was open for 1% of the time, Pallas kernels for 0%

profile of v1, /device:TPU:0, one launch (start us, length us, event | category | flops | bytes accessed | tf_op | source)
XLA Modules:
  0.0 305.4 jit_solution(2503206601856717499)
XLA Ops:
  7.4 19.6 %collective-permute-done = bf16[2,256,768]{2,1,0:T(8,128)(2,1)S(1)} collective-permute-done((bf16[2,256,768]{2,1,0:T(8,128)(2,1)S(1)}, bf16[2,256,768]{2,1,0:T(8,128)(2,1)S(1)}, u32[]{:S(2)}, u32[]{:S(2)}) %collective-permute-start) | collective-permute-done | bytes 786464 | tf_op jit(solution)/shard_map/ppermute | solution.py:19
  27.0 20.5 %collective-permute-done.1 = bf16[2,256,768]{2,1,0:T(8,128)(2,1)S(1)} collective-permute-done((bf16[2,256,768]{2,1,0:T(8,128)(2,1)S(1)}, bf16[2,256,768]{2,1,0:T(8,128)(2,1)S(1)}, u32[]{:S(2)}, u32[]{:S(2)}) %collective-permute-start.1) | collective-permute-done | bytes 786464 | tf_op jit(solution)/shard_map/ppermute | solution.py:19
  49.5 17.7 %collective-permute-done.2 = bf16[2,256,768]{2,1,0:T(8,128)(2,1)S(1)} collective-permute-done((bf16[2,256,768]{2,1,0:T(8,128)(2,1)S(1)}, bf16[2,256,768]{2,1,0:T(8,128)(2,1)S(1)}, u32[]{:S(2)}, u32[]{:S(2)}) %collective-permute-start.2) | collective-permute-done | bytes 786464 | tf_op jit(solution)/shard_map/ppermute | solution.py:19
  68.1 4.1 %multiply_reduce_fusion = (f32[]{:T(128)}, f32[768,768]{1,0:T(8,128)S(1)}) fusion(bf16[2,1024,768]{2,1,0:T(8,128)(2,1)} %constant_dynamic-update-slice_fusion.1, s32[]{:T(128)S(6)} %select_n.48), kind=kOutput, calls=%fused_computation.22 | convolution fusion | flops 1209729024 | bytes 3932168 | tf_op jit(solution)/shard_map/dot_general | solution.py:55
  72.9 163.0 %while.25 = (s32[]{:T(128)}, f32[4,768,256]{2,1,0:T(8,128)}, f32[4]{0:T(128)S(1)}, f32[4]{0:T(128)S(1)}, s32[4,768,256]{2,1,0:T(8,128)}, /*index=5*/bf16[4,768,2...) while((s32[]{:T(128)}, f32[4,768,256]{2,1,0:T(8,128)}, ...), condition=%wide.region_6.7_spmd, body=%wide.region_1.6_spmd.sunk | while | flops 5439750144 | bytes 29491652 | solution.py:65
  86.4 27.0 %while.26 = (s32[]{:T(128)}, f32[768,256]{0,1:T(8,128)S(1)}, s32[]{:T(128)}, f32[]{:T(128)}, f32[768,256]{0,1:T(8,128)}, /*index=5*/f32[768,768]{1,0:T(8,128)S(1)}, f32[]{:T(128)}, f32[768,256]{0,1:T(8,128)}, s32[]{:T(128)}) while((s32[]{:T(128)}, f32[768,256]{0,1:T(8,128)S(1)}, s32[]{:T(128)}, f32[]{:T(128)}, f32[768,256]{0,1:T(8,128)}, ...), condition=%wide.region_3.3_spmd, body=%wide.region_2.2_spmd.sunk | while | flops 1813118976 | bytes 7077989 | solution.py:36
  87.1 3.7 %fusion.38 = f32[768,256]{0,1:T(8,128)S(1)} fusion(f32[768,256]{0,1:T(8,128)S(1)} %copy.52, f32[768,256]{0,1:T(8,128)} %get-tuple-element.309, f32[768,768]{1,0:T(8,128)S(1)} %get-tuple-element.307, f32[768,256]{0,1:T(8,128)} %get-tuple-element.306, f32[]{:T(128)} %get-tuple-element.308, f32[]{:T(128)} %get-tuple-element.305), kind=kOutput, calls=%fused_computation.4.clone.1 | convolution fusion | flops 1813118976 | bytes 5505032 | tf_op jit(solution)/shard_map/while/body/eval_jaxpr/while/body/dot_general | solution.py:31
  91.5 3.7 %fusion.38 = f32[768,256]{0,1:T(8,128)S(1)} fusion(f32[768,256]{0,1:T(8,128)S(1)} %copy.52, f32[768,256]{0,1:T(8,128)} %get-tuple-element.309, f32[768,768]{1,0:T(8,128)S(1)} %get-tuple-element.307, f32[768,256]{0,1:T(8,128)} %get-tuple-element.306, f32[]{:T(128)} %get-tuple-element.308, f32[]{:T(128)} %get-tuple-element.305), kind=kOutput, calls=%fused_computation.4.clone.1 | convolution fusion | flops 1813118976 | bytes 5505032 | tf_op jit(solution)/shard_map/while/body/eval_jaxpr/while/body/dot_general | solution.py:31
  95.8 3.7 %fusion.38 = f32[768,256]{0,1:T(8,128)S(1)} fusion(f32[768,256]{0,1:T(8,128)S(1)} %copy.52, f32[768,256]{0,1:T(8,128)} %get-tuple-element.309, f32[768,768]{1,0:T(8,128)S(1)} %get-tuple-element.307, f32[768,256]{0,1:T(8,128)} %get-tuple-element.306, f32[]{:T(128)} %get-tuple-element.308, f32[]{:T(128)} %get-tuple-element.305), kind=kOutput, calls=%fused_computation.4.clone.1 | convolution fusion | flops 1813118976 | bytes 5505032 | tf_op jit(solution)/shard_map/while/body/eval_jaxpr/while/body/dot_general | solution.py:31
  100.2 3.7 %fusion.38 = f32[768,256]{0,1:T(8,128)S(1)} fusion(f32[768,256]{0,1:T(8,128)S(1)} %copy.52, f32[768,256]{0,1:T(8,128)} %get-tuple-element.309, f32[768,768]{1,0:T(8,128)S(1)} %get-tuple-element.307, f32[768,256]{0,1:T(8,128)} %get-tuple-element.306, f32[]{:T(128)} %get-tuple-element.308, f32[]{:T(128)} %get-tuple-element.305), kind=kOutput, calls=%fused_computation.4.clone.1 | convolution fusion | flops 1813118976 | bytes 5505032 | tf_op jit(solution)/shard_map/while/body/eval_jaxpr/while/body/dot_general | solution.py:31
  104.6 3.7 %fusion.38 = f32[768,256]{0,1:T(8,128)S(1)} fusion(f32[768,256]{0,1:T(8,128)S(1)} %copy.52, f32[768,256]{0,1:T(8,128)} %get-tuple-element.309, f32[768,768]{1,0:T(8,128)S(1)} %get-tuple-element.307, f32[768,256]{0,1:T(8,128)} %get-tuple-element.306, f32[]{:T(128)} %get-tuple-element.308, f32[]{:T(128)} %get-tuple-element.305), kind=kOutput, calls=%fused_computation.4.clone.1 | convolution fusion | flops 1813118976 | bytes 5505032 | tf_op jit(solution)/shard_map/while/body/eval_jaxpr/while/body/dot_general | solution.py:31
  109.0 3.7 %fusion.38 = f32[768,256]{0,1:T(8,128)S(1)} fusion(f32[768,256]{0,1:T(8,128)S(1)} %copy.52, f32[768,256]{0,1:T(8,128)} %get-tuple-element.309, f32[768,768]{1,0:T(8,128)S(1)} %get-tuple-element.307, f32[768,256]{0,1:T(8,128)} %get-tuple-element.306, f32[]{:T(128)} %get-tuple-element.308, f32[]{:T(128)} %get-tuple-element.305), kind=kOutput, calls=%fused_computation.4.clone.1 | convolution fusion | flops 1813118976 | bytes 5505032 | tf_op jit(solution)/shard_map/while/body/eval_jaxpr/while/body/dot_general | solution.py:31
  133.7 27.0 %while.26 = (s32[]{:T(128)}, f32[768,256]{0,1:T(8,128)S(1)}, s32[]{:T(128)}, f32[]{:T(128)}, f32[768,256]{0,1:T(8,128)}, /*index=5*/f32[768,768]{1,0:T(8,128)S(1)}, f32[]{:T(128)}, f32[768,256]{0,1:T(8,128)}, s32[]{:T(128)}) while((s32[]{:T(128)}, f32[768,256]{0,1:T(8,128)S(1)}, s32[]{:T(128)}, f32[]{:T(128)}, f32[768,256]{0,1:T(8,128)}, ...), condition=%wide.region_3.3_spmd, body=%wide.region_2.2_spmd.sunk | while | flops 1813118976 | bytes 7077989 | solution.py:36
  134.4 3.7 %fusion.38 = f32[768,256]{0,1:T(8,128)S(1)} fusion(f32[768,256]{0,1:T(8,128)S(1)} %copy.52, f32[768,256]{0,1:T(8,128)} %get-tuple-element.309, f32[768,768]{1,0:T(8,128)S(1)} %get-tuple-element.307, f32[768,256]{0,1:T(8,128)} %get-tuple-element.306, f32[]{:T(128)} %get-tuple-element.308, f32[]{:T(128)} %get-tuple-element.305), kind=kOutput, calls=%fused_computation.4.clone.1 | convolution fusion | flops 1813118976 | bytes 5505032 | tf_op jit(solution)/shard_map/while/body/eval_jaxpr/while/body/dot_general | solution.py:31
  138.8 3.7 %fusion.38 = f32[768,256]{0,1:T(8,128)S(1)} fusion(f32[768,256]{0,1:T(8,128)S(1)} %copy.52, f32[768,256]{0,1:T(8,128)} %get-tuple-element.309, f32[768,768]{1,0:T(8,128)S(1)} %get-tuple-element.307, f32[768,256]{0,1:T(8,128)} %get-tuple-element.306, f32[]{:T(128)} %get-tuple-element.308, f32[]{:T(128)} %get-tuple-element.305), kind=kOutput, calls=%fused_computation.4.clone.1 | convolution fusion | flops 1813118976 | bytes 5505032 | tf_op jit(solution)/shard_map/while/body/eval_jaxpr/while/body/dot_general | solution.py:31
  143.2 3.7 %fusion.38 = f32[768,256]{0,1:T(8,128)S(1)} fusion(f32[768,256]{0,1:T(8,128)S(1)} %copy.52, f32[768,256]{0,1:T(8,128)} %get-tuple-element.309, f32[768,768]{1,0:T(8,128)S(1)} %get-tuple-element.307, f32[768,256]{0,1:T(8,128)} %get-tuple-element.306, f32[]{:T(128)} %get-tuple-element.308, f32[]{:T(128)} %get-tuple-element.305), kind=kOutput, calls=%fused_computation.4.clone.1 | convolution fusion | flops 1813118976 | bytes 5505032 | tf_op jit(solution)/shard_map/while/body/eval_jaxpr/while/body/dot_general | solution.py:31
  147.6 3.7 %fusion.38 = f32[768,256]{0,1:T(8,128)S(1)} fusion(f32[768,256]{0,1:T(8,128)S(1)} %copy.52, f32[768,256]{0,1:T(8,128)} %get-tuple-element.309, f32[768,768]{1,0:T(8,128)S(1)} %get-tuple-element.307, f32[768,256]{0,1:T(8,128)} %get-tuple-element.306, f32[]{:T(128)} %get-tuple-element.308, f32[]{:T(128)} %get-tuple-element.305), kind=kOutput, calls=%fused_computation.4.clone.1 | convolution fusion | flops 1813118976 | bytes 5505032 | tf_op jit(solution)/shard_map/while/body/eval_jaxpr/while/body/dot_general | solution.py:31
  152.0 3.7 %fusion.38 = f32[768,256]{0,1:T(8,128)S(1)} fusion(f32[768,256]{0,1:T(8,128)S(1)} %copy.52, f32[768,256]{0,1:T(8,128)} %get-tuple-element.309, f32[768,768]{1,0:T(8,128)S(1)} %get-tuple-element.307, f32[768,256]{0,1:T(8,128)} %get-tuple-element.306, f32[]{:T(128)} %get-tuple-element.308, f32[]{:T(128)} %get-tuple-element.305), kind=kOutput, calls=%fused_computation.4.clone.1 | convolution fusion | flops 1813118976 | bytes 5505032 | tf_op jit(solution)/shard_map/while/body/eval_jaxpr/while/body/dot_general | solution.py:31
  181.0 13.8 %while.26 = (s32[]{:T(128)}, f32[768,256]{0,1:T(8,128)S(1)}, s32[]{:T(128)}, f32[]{:T(128)}, f32[768,256]{0,1:T(8,128)}, /*index=5*/f32[768,768]{1,0:T(8,128)S(1)}, f32[]{:T(128)}, f32[768,256]{0,1:T(8,128)}, s32[]{:T(128)}) while((s32[]{:T(128)}, f32[768,256]{0,1:T(8,128)S(1)}, s32[]{:T(128)}, f32[]{:T(128)}, f32[768,256]{0,1:T(8,128)}, ...), condition=%wide.region_3.3_spmd, body=%wide.region_2.2_spmd.sunk | while | flops 1813118976 | bytes 7077989 | solution.py:36
  190.5 3.7 %fusion.38 = f32[768,256]{0,1:T(8,128)S(1)} fusion(f32[768,256]{0,1:T(8,128)S(1)} %copy.52, f32[768,256]{0,1:T(8,128)} %get-tuple-element.309, f32[768,768]{1,0:T(8,128)S(1)} %get-tuple-element.307, f32[768,256]{0,1:T(8,128)} %get-tuple-element.306, f32[]{:T(128)} %get-tuple-element.308, f32[]{:T(128)} %get-tuple-element.305), kind=kOutput, calls=%fused_computation.4.clone.1 | convolution fusion | flops 1813118976 | bytes 5505032 | tf_op jit(solution)/shard_map/while/body/eval_jaxpr/while/body/dot_general | solution.py:31
  215.2 13.8 %while.26 = (s32[]{:T(128)}, f32[768,256]{0,1:T(8,128)S(1)}, s32[]{:T(128)}, f32[]{:T(128)}, f32[768,256]{0,1:T(8,128)}, /*index=5*/f32[768,768]{1,0:T(8,128)S(1)}, f32[]{:T(128)}, f32[768,256]{0,1:T(8,128)}, s32[]{:T(128)}) while((s32[]{:T(128)}, f32[768,256]{0,1:T(8,128)S(1)}, s32[]{:T(128)}, f32[]{:T(128)}, f32[768,256]{0,1:T(8,128)}, ...), condition=%wide.region_3.3_spmd, body=%wide.region_2.2_spmd.sunk | while | flops 1813118976 | bytes 7077989 | solution.py:36
  220.3 3.7 %fusion.38 = f32[768,256]{0,1:T(8,128)S(1)} fusion(f32[768,256]{0,1:T(8,128)S(1)} %copy.52, f32[768,256]{0,1:T(8,128)} %get-tuple-element.309, f32[768,768]{1,0:T(8,128)S(1)} %get-tuple-element.307, f32[768,256]{0,1:T(8,128)} %get-tuple-element.306, f32[]{:T(128)} %get-tuple-element.308, f32[]{:T(128)} %get-tuple-element.305), kind=kOutput, calls=%fused_computation.4.clone.1 | convolution fusion | flops 1813118976 | bytes 5505032 | tf_op jit(solution)/shard_map/while/body/eval_jaxpr/while/body/dot_general | solution.py:31
  237.7 8.3 %psum.14 = f32[2]{0:T(128)S(1)} all-reduce(f32[2]{0:T(128)S(1)} %compare_select_fusion), channel_id=1, replica_groups=mesh['expert'=8,'token'=4] {'token'}, use_global_device_ids=true, to_apply=%region_8.9 | all-reduce | flops 2 | bytes 16 | tf_op jit(solution)/shard_map/psum | solution.py:69
  246.1 58.1 %psum.15 = f32[]{:T(128)} all-reduce(f32[]{:T(128)} %reduce_sum.47), channel_id=1, replica_groups=mesh['expert'=8,'token'=4] {'expert','token'}, use_global_device_ids=true, to_apply=%region_10.11 | all-reduce | flops 1 | bytes 8 | tf_op jit(solution)/shard_map/psum | solution.py:70
  (113 shorter events, 110.3 us)
Async XLA Ops:
  0.6 2.7 copy-start.1
  4.3 22.7 %collective-permute-start = (bf16[2,256,768]{2,1,0:T(8,128)(2,1)S(1)}, bf16[2,256,768]{2,1,0:T(8,128)(2,1)S(1)}, u32[]{:S(2)}, u32[]{:S(2)}) collective-permute-start(bf16[2,256,768]{2,1,0:T(8,128)(2,1)S(1)} %get-tuple-element.151), channel_id=1, source_target_pairs={{0,1},{1,2},{2,3},{3,0},{4,5},{5,6},{6,7},{7,4},{8,9},{9,10},{10,1... | collective-permute-start | bytes 2359304 | tf_op jit(solution)/shard_map/ppermute | solution.py:19
  27.0 20.5 %collective-permute-start.1 = (bf16[2,256,768]{2,1,0:T(8,128)(2,1)S(1)}, bf16[2,256,768]{2,1,0:T(8,128)(2,1)S(1)}, u32[]{:S(2)}, u32[]{:S(2)}) collective-permute-start(bf16[2,256,768]{2,1,0:T(8,128)(2,1)S(1)} %collective-permute-done), channel_id=1, source_target_pairs={{0,1},{1,2},{2,3},{3,0},{4,5},{5,6},{6,7},{7,4},{8,9},{9,10},{10,1... | collective-permute-start | bytes 2359304 | tf_op jit(solution)/shard_map/ppermute | solution.py:19
  47.5 19.6 %collective-permute-start.2 = (bf16[2,256,768]{2,1,0:T(8,128)(2,1)S(1)}, bf16[2,256,768]{2,1,0:T(8,128)(2,1)S(1)}, u32[]{:S(2)}, u32[]{:S(2)}) collective-permute-start(bf16[2,256,768]{2,1,0:T(8,128)(2,1)S(1)} %collective-permute-done.1), channel_id=1, source_target_pairs={{0,1},{1,2},{2,3},{3,0},{4,5},{5,6},{6,7},{7,4},{8,9},{9,10},{10,1... | collective-permute-start | bytes 2359304 | tf_op jit(solution)/shard_map/ppermute | solution.py:19
  49.5 23.4 %copy-start.2 = (s32[4]{0:T(128)S(1)}, s32[4]{0:T(128)}, u32[]{:S(2)}) copy-start(s32[4]{0:T(128)} %param.14) | copy-start | bytes 52
  49.5 23.4 %copy-start.3 = (f32[4]{0:T(128)S(1)}, f32[4]{0:T(128)}, u32[]{:S(2)}) copy-start(f32[4]{0:T(128)} %param.15) | copy-start | bytes 52
  83.3 0.9 copy-start
  130.6 0.9 copy-start
  178.0 0.9 copy-start
  212.1 0.9 copy-start
